TPU v7x, 512 devices: a whole 4x4x16 slice. The times are simulated.
512 devices in a mesh: loop: 64 (over z, x_hi, core), narrow: 8 (over x_lo, y).
Axes of the slice: x: 4 (x_hi: 2, x_lo: 2; x = x_hi * 2 + x_lo), y: 4, z: 16, core: 2. Of those that a mesh axis runs over, the one named last changes fastest.
Arguments:
- tokens: bfloat16 [1024, 8192], P('loop', 'narrow'), may hold values from -6 to 6
- gate_weight: bfloat16 [8192, 28672], P('narrow', 'loop'), may hold values from -0.0625 to 0.0625
- up_weight: bfloat16 [8192, 28672], P('narrow', 'loop'), may hold values from -0.0625 to 0.0625
- down_weight: bfloat16 [28672, 8192], P('loop', 'narrow'), may hold values from -0.03125 to 0.03125
Outputs:
- mixed: bfloat16 [1024, 8192], P('loop', 'narrow')
All inputs are finite; a program needn't handle non-finite values.
Results may differ from a plain program's by a relative error of at most 0.0049.
Values may be sent and summed in bfloat16 or wider, within the bound.
No kernel may reach another device: no remote copies, remote signals or barrier semaphores. Data moves between devices by JAX's collectives and lax.ppermute only.
A program may use at most 64 MiB of HBM per device.

v0:
```python
import jax
import jax.numpy as jnp
from jax import lax
from jax.sharding import Mesh, PartitionSpec as P

AXES = ("zh", "zl", "xh", "core", "xl", "y")
Z = ("zh", "zl")
NARROW = ("xl", "y")
SWAP = [(0, 1), (1, 0)]


def f32dot(a, b):
    return jnp.dot(a, b, preferred_element_type=jnp.float32)


def shards(tokens, gate_weight, up_weight, down_weight):
    gate_other = lax.ppermute(gate_weight, "core", SWAP)
    up_other = lax.ppermute(up_weight, "core", SWAP)
    down_other = lax.ppermute(down_weight, "core", SWAP)
    rows = lax.all_gather(tokens, Z, axis=0, tiled=True)
    near = lax.all_to_all(jnp.broadcast_to(rows, (2, *rows.shape)), "xh", 0, 0)
    rows = near.reshape(-1, tokens.shape[1])
    n_rows = rows.shape[0]
    gates = jnp.concatenate((gate_weight, gate_other), axis=1)
    ups = jnp.concatenate((up_weight, up_other), axis=1)
    width = gates.shape[1]
    partial = jnp.concatenate(
        (f32dot(rows, gates).astype(jnp.bfloat16), f32dot(rows, ups).astype(jnp.bfloat16)), axis=1
    )
    partial = partial.reshape(8, n_rows // 8, 2 * width)
    parts = lax.all_to_all(partial, NARROW, 0, 0)
    totals = jnp.sum(parts.astype(jnp.float32), axis=0)
    hidden = (jax.nn.silu(totals[:, :width]) * totals[:, width:]).astype(jnp.bfloat16)
    hidden = lax.all_to_all(jnp.broadcast_to(hidden, (8, *hidden.shape)), NARROW, 0, 0)
    hidden = hidden.reshape(n_rows, width)
    downs = jnp.concatenate((down_weight, down_other), axis=0)
    mixed = f32dot(hidden, downs).astype(jnp.bfloat16)
    mixed = mixed.reshape(2, 4, 4, 16, -1)
    mixed = mixed.transpose(2, 0, 1, 3, 4).reshape(8, 64, -1)
    mixed = lax.all_to_all(mixed, ("zl", "xh"), 0, 0)
    mixed = jnp.sum(mixed.astype(jnp.float32), axis=0).astype(jnp.bfloat16)
    mixed = lax.all_to_all(mixed.reshape(4, 16, -1), "zh", 0, 0)
    return jnp.sum(mixed.astype(jnp.float32), axis=0).astype(jnp.bfloat16)


def solution(mesh):
    fine = Mesh(mesh.devices.reshape(4, 4, 2, 2, 2, 4), AXES)
    loop, narrow = (("zh", "zl", "xh", "core"), NARROW)
    return jax.shard_map(
        shards,
        mesh=fine,
        in_specs=(P(loop, narrow), P(narrow, loop), P(narrow, loop), P(loop, narrow)),
        out_specs=P(loop, narrow),
        check_vma=False,
    )
```

profile of v0, /device:TPU:2, one launch (start us, length us, event | category | flops | bytes accessed | tf_op | source)
XLA Modules:
  0.0 147.9 jit_solution(17875800447940083722)
XLA Ops:
  0.0 1.9 %collective-permute-start = (bf16[1024,448]{0,1:T(8,128)(2,1)}, bf16[1024,448]{0,1:T(8,128)(2,1)S(1)}, u32[]{:S(2)}, u32[]{:S(2)}) collective-permute-start(bf16[1024,448]{0,1:T(8,128)(2,1)} %param.5), channel_id=1, source_target_pairs={{0,8},{8,0},{1,9},{9,1},{2,10},{10,2},{3,11},{11,3},{4,12},{12,4},... | collective-permute-start | bytes 2752520 | tf_op jit(solution)/shard_map/ppermute | solution.py:17
  1.9 2.4 %collective-permute-start.1 = (bf16[1024,448]{0,1:T(8,128)(2,1)}, bf16[1024,448]{0,1:T(8,128)(2,1)S(1)}, u32[]{:S(2)}, u32[]{:S(2)}) collective-permute-start(bf16[1024,448]{0,1:T(8,128)(2,1)} %param.6), channel_id=1, source_target_pairs={{0,8},{8,0},{1,9},{9,1},{2,10},{10,2},{3,11},{11,3},{4,12},{12,4},... | collective-permute-start | bytes 2752520 | tf_op jit(solution)/shard_map/ppermute | solution.py:18
  4.3 38.8 %all_gather.3 = bf16[256,1024]{1,0:T(8,128)(2,1)S(1)} all-gather(bf16[16,1024]{1,0:T(8,128)(2,1)} %param.4), channel_id=1, replica_groups=mesh['zh'=4,'zl'=4,'xh'=2,'core'=2,'xl'=2,'y'=4] {'zh','zl'}, dimensions={0}, use_global_device_ids=true | all-gather | bytes 557056 | tf_op jit(solution)/shard_map/all_gather | solution.py:20
  43.2 0.0 copy-start
  43.2 0.1 broadcast_in_dim.6
  43.3 14.2 %all_to_all.25 = bf16[2,256,1024]{2,1,0:T(8,128)(2,1)S(1)} all-to-all(bf16[2,256,1024]{2,1,0:T(8,128)(2,1)S(1)} %broadcast_in_dim.6), channel_id=1, replica_groups=mesh['zh'=4,'zl'=4,'xh'=2,'core'=2,'xl'=2,'y'=4] {'xh'}, dimensions={0} | all-to-all | bytes 2097152 | tf_op jit(solution)/shard_map/all_to_all | solution.py:21
  57.5 0.0 collective-permute-done
  57.5 0.0 copy-done
  57.5 0.0 copy-start.1
  57.5 1.1 fusion.21
  58.7 0.0 collective-permute-done.1
  58.7 0.0 copy-done.1
  58.7 1.1 fusion.24
  59.8 0.1 pad_maximum_fusion
  60.0 2.5 %copy.7 = bf16[512,1792]{1,0:T(8,128)(2,1)} copy(bf16[512,1792]{0,1:T(8,128)(2,1)S(1)} %pad_maximum_fusion) | data formatting | bytes 3670016 | tf_op jit(solution)/shard_map/concatenate | solution.py:27
  62.4 0.0 copy-start.2
  62.4 6.1 %all-to-all-start.1 = ((bf16[8,64,1792]{2,1,0:T(8,128)(2,1)}), bf16[8,64,1792]{2,1,0:T(8,128)(2,1)S(1)}, u32[]{:S(2)}, u32[]{:S(2)}) async-start(bf16[8,64,1792]{2,1,0:T(8,128)(2,1)} %bitcast.3), calls=%async_computation.1 | async-start | bytes 3670016 | tf_op jit(solution)/shard_map/all_to_all | solution.py:31
  68.5 0.0 copy-done.2
  68.5 1.9 %collective-permute-start.2 = (bf16[448,1024]{1,0:T(8,128)(2,1)S(1)}, bf16[448,1024]{1,0:T(8,128)(2,1)}, u32[]{:S(2)}, u32[]{:S(2)}) collective-permute-start(bf16[448,1024]{1,0:T(8,128)(2,1)S(1)} %copy-done.2), channel_id=1, source_target_pairs={{0,8},{8,0},{1,9},{9,1},{2,10},{10,2},{3,11},{11,3},{4,12},{12,4},... | collective-permute-start | bytes 2752520 | tf_op jit(solution)/shard_map/ppermute | solution.py:19
  70.4 12.6 %all-to-all-done.1 = bf16[8,64,1792]{2,1,0:T(8,128)(2,1)S(1)} async-done(((bf16[8,64,1792]{2,1,0:T(8,128)(2,1)}), bf16[8,64,1792]{2,1,0:T(8,128)(2,1)S(1)}, u32[]{:S(2)}, u32[]{:S(2)}) %all-to-all-start.1) | async-done | bytes 1835040 | tf_op jit(solution)/shard_map/all_to_all | solution.py:31
  83.0 0.2 convert_reduce_fusion
  83.3 0.1 fusion.27
  83.3 1.0 broadcast_in_dim.7
  84.4 4.3 %all-to-all-start.2 = ((bf16[8,64,896]{2,1,0:T(8,128)(2,1)}), bf16[8,64,896]{2,1,0:T(8,128)(2,1)S(1)}, u32[]{:S(2)}, u32[]{:S(2)}) async-start(bf16[8,64,896]{2,1,0:T(8,128)(2,1)} %broadcast_in_dim.7), calls=%async_computation.2 | async-start | bytes 1835008 | tf_op jit(solution)/shard_map/all_to_all | solution.py:34
  88.7 0.0 collective-permute-done.2
  88.7 9.3 %all-to-all-done.2 = bf16[8,64,896]{2,1,0:T(8,128)(2,1)S(1)} async-done(((bf16[8,64,896]{2,1,0:T(8,128)(2,1)}), bf16[8,64,896]{2,1,0:T(8,128)(2,1)S(1)}, u32[]{:S(2)}, u32[]{:S(2)}) %all-to-all-start.2) | async-done | bytes 917536 | tf_op jit(solution)/shard_map/all_to_all | solution.py:34
  98.1 2.4 %fusion.12 = bf16[512,1024]{1,0:T(8,128)(2,1)S(1)} fusion(bf16[512,896]{1,0:T(8,128)(2,1)S(1)} %bitcast.19, bf16[448,1024]{1,0:T(8,128)(2,1)} %collective-permute-done.2, bf16[448,1024]{1,0:T(8,128)(2,1)S(1)} %copy-done.2), kind=kOutput, calls=%fused_computation.14 | convolution fusion | flops 943718400 | bytes 3801088 | tf_op jit(solution)/shard_map/dot_general | solution.py:13
  100.5 0.1 copy.8
  100.6 23.7 %all_to_all.26 = bf16[8,64,1024]{2,1,0:T(8,128)(2,1)S(1)} all-to-all(bf16[8,64,1024]{2,1,0:T(8,128)(2,1)S(1)} %bitcast.15), channel_id=1, replica_groups=mesh['zh'=4,'zl'=4,'xh'=2,'core'=2,'xl'=2,'y'=4] {'zl','xh'}, dimensions={0} | all-to-all | bytes 2097152 | tf_op jit(solution)/shard_map/all_to_all | solution.py:40
  124.3 0.2 reduce_sum.34
  124.5 22.8 %all_to_all.27 = bf16[4,16,1024]{2,1,0:T(8,128)(2,1)S(1)} all-to-all(bf16[4,16,1024]{2,1,0:T(8,128)(2,1)S(1)} %bitcast.20), channel_id=1, replica_groups=mesh['zh'=4,'zl'=4,'xh'=2,'core'=2,'xl'=2,'y'=4] {'zh'}, dimensions={0} | all-to-all | bytes 262144 | tf_op jit(solution)/shard_map/all_to_all | solution.py:42
  147.3 0.6 reduce_sum.35
Async XLA Ops:
  0.0 57.5 %collective-permute-start = (bf16[1024,448]{0,1:T(8,128)(2,1)}, bf16[1024,448]{0,1:T(8,128)(2,1)S(1)}, u32[]{:S(2)}, u32[]{:S(2)}) collective-permute-start(bf16[1024,448]{0,1:T(8,128)(2,1)} %param.5), channel_id=1, source_target_pairs={{0,8},{8,0},{1,9},{9,1},{2,10},{10,2},{3,11},{11,3},{4,12},{12,4},... | collective-permute-start | bytes 2752520 | tf_op jit(solution)/shard_map/ppermute | solution.py:17
  1.9 56.8 %collective-permute-start.1 = (bf16[1024,448]{0,1:T(8,128)(2,1)}, bf16[1024,448]{0,1:T(8,128)(2,1)S(1)}, u32[]{:S(2)}, u32[]{:S(2)}) collective-permute-start(bf16[1024,448]{0,1:T(8,128)(2,1)} %param.6), channel_id=1, source_target_pairs={{0,8},{8,0},{1,9},{9,1},{2,10},{10,2},{3,11},{11,3},{4,12},{12,4},... | collective-permute-start | bytes 2752520 | tf_op jit(solution)/shard_map/ppermute | solution.py:18
  43.2 14.4 %copy-start = (bf16[1024,448]{0,1:T(8,128)(2,1)S(1)}, bf16[1024,448]{0,1:T(8,128)(2,1)}, u32[]{:S(2)}) copy-start(bf16[1024,448]{0,1:T(8,128)(2,1)} %param.5) | copy-start | bytes 2752516
  57.5 1.2 copy-start.1
  62.4 6.1 %copy-start.2 = (bf16[448,1024]{1,0:T(8,128)(2,1)S(1)}, bf16[448,1024]{1,0:T(8,128)(2,1)}, u32[]{:S(2)}) copy-start(bf16[448,1024]{1,0:T(8,128)(2,1)} %param.7) | copy-start | bytes 2752516
  62.4 20.6 %all-to-all-start.1 = ((bf16[8,64,1792]{2,1,0:T(8,128)(2,1)}), bf16[8,64,1792]{2,1,0:T(8,128)(2,1)S(1)}, u32[]{:S(2)}, u32[]{:S(2)}) async-start(bf16[8,64,1792]{2,1,0:T(8,128)(2,1)} %bitcast.3), calls=%async_computation.1 | async-start | bytes 3670016 | tf_op jit(solution)/shard_map/all_to_all | solution.py:31
  68.5 20.2 %collective-permute-start.2 = (bf16[448,1024]{1,0:T(8,128)(2,1)S(1)}, bf16[448,1024]{1,0:T(8,128)(2,1)}, u32[]{:S(2)}, u32[]{:S(2)}) collective-permute-start(bf16[448,1024]{1,0:T(8,128)(2,1)S(1)} %copy-done.2), channel_id=1, source_target_pairs={{0,8},{8,0},{1,9},{9,1},{2,10},{10,2},{3,11},{11,3},{4,12},{12,4},... | collective-permute-start | bytes 2752520 | tf_op jit(solution)/shard_map/ppermute | solution.py:19
  84.4 13.7 %all-to-all-start.2 = ((bf16[8,64,896]{2,1,0:T(8,128)(2,1)}), bf16[8,64,896]{2,1,0:T(8,128)(2,1)S(1)}, u32[]{:S(2)}, u32[]{:S(2)}) async-start(bf16[8,64,896]{2,1,0:T(8,128)(2,1)} %broadcast_in_dim.7), calls=%async_computation.2 | async-start | bytes 1835008 | tf_op jit(solution)/shard_map/all_to_all | solution.py:34
where the time goes:
time: 148 us
  blocking collectives  99.5 us (67%)
  waiting for transfers between devices  21.9 us (15%)
  starting transfers between devices  16.6 us (11%)
  matrix products  4.72 us (3%)
  local copies, waits for them, and re-layouts  3.77 us (3%)
    all_gather x1, blocking collectives, shards(): rows = lax.all_gather(tokens, Z, axis=0, tiled=True)  38.8 us
    all_to_all x1, blocking collectives, shards(): mixed = lax.all_to_all(mixed, ('zl', 'xh'), 0, 0)  23.7 us
    all_to_all x1, blocking collectives, shards(): mixed = lax.all_to_all(mixed.reshape(4, 16, -1), 'zh', 0, 0)  22.8 us
    all_to_all x1, blocking collectives, shards(): near = lax.all_to_all(jnp.broadcast_to(rows, (2, *rows.shape)), 'xh', 0, 0)  14.2 us
    all_to_all x1, waiting for transfers between devices, shards(): parts = lax.all_to_all(partial, NARROW, 0, 0)  12.6 us
    all_to_all x1, waiting for transfers between devices, shards(): lax.all_to_all(jnp.broadcast_to(hidden, (8, *hidden.shape)), NARROW, 0, 0)  9.33 us
    all_to_all x1, starting transfers between devices, shards(): parts = lax.all_to_all(partial, NARROW, 0, 0)  6.06 us
    dot_general x3, matrix products, f32dot(): return jnp.dot(a, b, preferred_element_type=jnp.float32)  4.72 us
  transfers between devices with their start and end apart: 5, of which 2 were waited for; matrix products, arithmetic and copies ran while one was open for 2% of the time, Pallas kernels for 0%

commit v1 on v0

--- a/solution.py
+++ b/solution.py
@@ -17,7 +17,7 @@
     gate_other = lax.ppermute(gate_weight, "core", SWAP)
     up_other = lax.ppermute(up_weight, "core", SWAP)
     down_other = lax.ppermute(down_weight, "core", SWAP)
-    rows = lax.all_gather(tokens, Z, axis=0, tiled=True)
+    rows = jnp.concatenate(lax.all_to_all(jnp.stack([tokens] * lax.axis_size(Z)), Z, 0, 0), axis=0)
     near = lax.all_to_all(jnp.broadcast_to(rows, (2, *rows.shape)), "xh", 0, 0)
     rows = near.reshape(-1, tokens.shape[1])
     n_rows = rows.shape[0]

time: 148 us -> 173 us (1.17)
  waiting for transfers between devices: 21.9 us -> 59.2 us
  blocking collectives: 99.5 us -> 63.7 us
  starting transfers between devices: 16.6 us -> 35.4 us
  local copies, waits for them, and re-layouts: 3.77 us -> 6.37 us
    all_gather x1 -> x0, blocking collectives: 38.8 us -> none  [shards(): rows = lax.all_gather(tokens, Z, axis=0, tiled=True)]
    all_to_all x0 -> x2, waiting for transfers between devices: none -> 35.6 us  [the longest x1 24.7 us: shards(): lax.all_to_all(jnp.stack([tokens] * lax.axis_size(Z)), Z, 0, 0)]
    all_to_all x0 -> x2, starting transfers between devices: none -> 18.8 us  [the longest x1 15.2 us: shards(): lax.all_to_all(jnp.stack([tokens] * lax.axis_size(Z)), Z, 0, 0)]
    all_to_all x1 -> x0, blocking collectives: 14.2 us -> none  [shards(): near = lax.all_to_all(jnp.broadcast_to(rows, (2, *rows.shape)), 'xh', 0, 0)]
    all_to_all x1, blocking collectives: 23.7 us -> 36.7 us  [shards(): mixed = lax.all_to_all(mixed, ('zl', 'xh'), 0, 0)]
    all_to_all x1, blocking collectives: 22.8 us -> 27 us  [shards(): mixed = lax.all_to_all(mixed.reshape(4, 16, -1), 'zh', 0, 0)]
  transfers between devices with their start and end apart: 5 -> 7, of which waited for: 2 -> 4; matrix products, arithmetic and copies ran while one was open for 2% -> 3% of each run, Pallas kernels for 0% -> 0%
where the time goes in v1:
time: 173 us; the launch traced here: 172 us
  blocking collectives  63.7 us (37%)
  waiting for transfers between devices  59.2 us (34%)
  starting transfers between devices  35.4 us (20%)
  local copies, waits for them, and re-layouts  6.37 us (4%)
  matrix products  5.98 us (3%)
    all_to_all x1, blocking collectives, shards(): mixed = lax.all_to_all(mixed, ('zl', 'xh'), 0, 0)  36.7 us
    all_to_all x1, blocking collectives, shards(): mixed = lax.all_to_all(mixed.reshape(4, 16, -1), 'zh', 0, 0)  27 us
    all_to_all x1, waiting for transfers between devices, shards(): lax.all_to_all(jnp.stack([tokens] * lax.axis_size(Z)), Z, 0, 0)  24.7 us
    all_to_all x1, starting transfers between devices, shards(): lax.all_to_all(jnp.stack([tokens] * lax.axis_size(Z)), Z, 0, 0)  15.2 us
    all_to_all x1, waiting for transfers between devices, shards(): parts = lax.all_to_all(partial, NARROW, 0, 0)  13.1 us
    all_to_all x1, waiting for transfers between devices, shards(): near = lax.all_to_all(jnp.broadcast_to(rows, (2, *rows.shape)), 'xh', 0, 0)  10.9 us
    all_to_all x1, waiting for transfers between devices, shards(): lax.all_to_all(jnp.broadcast_to(hidden, (8, *hidden.shape)), NARROW, 0, 0)  10.6 us
    all_to_all x1, starting transfers between devices, shards(): parts = lax.all_to_all(partial, NARROW, 0, 0)  6.05 us
  transfers between devices with their start and end apart: 7, of which 4 were waited for; matrix products, arithmetic and copies ran while one was open for 3% of the time, Pallas kernels for 0%

profile of v1, /device:TPU:2, one launch (start us, length us, event | category | flops | bytes accessed | tf_op | source)
XLA Modules:
  0.0 172.0 jit_solution(11887927216656544281)
XLA Ops:
  0.0 1.6 stack.2
  1.6 15.2 %all-to-all-start = ((bf16[16,16,1024]{2,1,0:T(8,128)(2,1)}), bf16[16,16,1024]{2,1,0:T(8,128)(2,1)S(1)}, u32[]{:S(2)}, u32[]{:S(2)}) async-start(bf16[16,16,1024]{2,1,0:T(8,128)(2,1)} %stack.2), calls=%async_computation | async-start | bytes 1048576 | tf_op jit(solution)/shard_map/all_to_all | solution.py:20
  16.8 1.9 %collective-permute-start = (bf16[1024,448]{0,1:T(8,128)(2,1)}, bf16[1024,448]{0,1:T(8,128)(2,1)}, u32[]{:S(2)}, u32[]{:S(2)}) collective-permute-start(bf16[1024,448]{0,1:T(8,128)(2,1)} %param.5), channel_id=1, source_target_pairs={{0,8},{8,0},{1,9},{9,1},{2,10},{10,2},{3,11},{11,3},{4,12},{12,4},... | collective-permute-start | bytes 2752520 | tf_op jit(solution)/shard_map/ppermute | solution.py:17
  18.7 2.4 %collective-permute-start.1 = (bf16[1024,448]{0,1:T(8,128)(2,1)}, bf16[1024,448]{0,1:T(8,128)(2,1)S(1)}, u32[]{:S(2)}, u32[]{:S(2)}) collective-permute-start(bf16[1024,448]{0,1:T(8,128)(2,1)} %param.6), channel_id=1, source_target_pairs={{0,8},{8,0},{1,9},{9,1},{2,10},{10,2},{3,11},{11,3},{4,12},{12,4},... | collective-permute-start | bytes 2752520 | tf_op jit(solution)/shard_map/ppermute | solution.py:18
  21.2 24.7 %all-to-all-done = bf16[16,16,1024]{2,1,0:T(8,128)(2,1)S(1)} async-done(((bf16[16,16,1024]{2,1,0:T(8,128)(2,1)}), bf16[16,16,1024]{2,1,0:T(8,128)(2,1)S(1)}, u32[]{:S(2)}, u32[]{:S(2)}) %all-to-all-start) | async-done | bytes 524320 | tf_op jit(solution)/shard_map/all_to_all | solution.py:20
  45.9 0.0 copy-start
  45.9 1.1 broadcast_in_dim.6
  47.0 3.6 %all-to-all-start.1 = ((bf16[2,256,1024]{2,1,0:T(8,128)(2,1)}), bf16[2,256,1024]{2,1,0:T(8,128)(2,1)S(1)}, u32[]{:S(2)}, u32[]{:S(2)}) async-start(bf16[2,256,1024]{2,1,0:T(8,128)(2,1)} %broadcast_in_dim.6), calls=%async_computation.1 | async-start | bytes 2097152 | tf_op jit(solution)/shard_map/all_to_all | solution.py:21
  50.6 0.0 collective-permute-done
  50.6 10.9 %all-to-all-done.1 = bf16[2,256,1024]{2,1,0:T(8,128)(2,1)S(1)} async-done(((bf16[2,256,1024]{2,1,0:T(8,128)(2,1)}), bf16[2,256,1024]{2,1,0:T(8,128)(2,1)S(1)}, u32[]{:S(2)}, u32[]{:S(2)}) %all-to-all-start.1) | async-done | bytes 1048608 | tf_op jit(solution)/shard_map/all_to_all | solution.py:21
  61.5 0.0 copy-done
  61.5 0.0 copy-start.1
  61.5 2.4 %fusion.21 = bf16[512,896]{0,1:T(8,128)(2,1)S(1)} fusion(bf16[512,1024]{1,0:T(8,128)(2,1)S(1)} %bitcast.18, bf16[1024,448]{0,1:T(8,128)(2,1)} %collective-permute-done, bf16[1024,448]{0,1:T(8,128)(2,1)S(1)} %copy-done), kind=kOutput, calls=%fused_computation.17 | convolution fusion | flops 943652864 | bytes 3801088 | tf_op jit(solution)/shard_map/dot_general | solution.py:13
  63.9 0.0 collective-permute-done.1
  63.9 0.0 copy-done.1
  63.9 1.1 fusion.24
  65.1 0.1 pad_maximum_fusion
  65.2 2.5 %copy.7 = bf16[512,1792]{1,0:T(8,128)(2,1)} copy(bf16[512,1792]{0,1:T(8,128)(2,1)S(1)} %pad_maximum_fusion) | data formatting | bytes 3670016 | tf_op jit(solution)/shard_map/concatenate | solution.py:27
  67.7 0.0 copy-start.2
  67.7 6.1 %all-to-all-start.2 = ((bf16[8,64,1792]{2,1,0:T(8,128)(2,1)}), bf16[8,64,1792]{2,1,0:T(8,128)(2,1)S(1)}, u32[]{:S(2)}, u32[]{:S(2)}) async-start(bf16[8,64,1792]{2,1,0:T(8,128)(2,1)} %bitcast.4), calls=%async_computation.2 | async-start | bytes 3670016 | tf_op jit(solution)/shard_map/all_to_all | solution.py:31
  73.7 0.0 copy-done.2
  73.7 1.9 %collective-permute-start.2 = (bf16[448,1024]{1,0:T(8,128)(2,1)S(1)}, bf16[448,1024]{1,0:T(8,128)(2,1)}, u32[]{:S(2)}, u32[]{:S(2)}) collective-permute-start(bf16[448,1024]{1,0:T(8,128)(2,1)S(1)} %copy-done.2), channel_id=1, source_target_pairs={{0,8},{8,0},{1,9},{9,1},{2,10},{10,2},{3,11},{11,3},{4,12},{12,4},... | collective-permute-start | bytes 2752520 | tf_op jit(solution)/shard_map/ppermute | solution.py:19
  75.7 13.1 %all-to-all-done.2 = bf16[8,64,1792]{2,1,0:T(8,128)(2,1)S(1)} async-done(((bf16[8,64,1792]{2,1,0:T(8,128)(2,1)}), bf16[8,64,1792]{2,1,0:T(8,128)(2,1)S(1)}, u32[]{:S(2)}, u32[]{:S(2)}) %all-to-all-start.2) | async-done | bytes 1835040 | tf_op jit(solution)/shard_map/all_to_all | solution.py:31
  88.7 0.2 convert_reduce_fusion
  89.0 0.1 fusion.27
  89.0 1.1 broadcast_in_dim.7
  90.1 4.3 %all-to-all-start.3 = ((bf16[8,64,896]{2,1,0:T(8,128)(2,1)}), bf16[8,64,896]{2,1,0:T(8,128)(2,1)S(1)}, u32[]{:S(2)}, u32[]{:S(2)}) async-start(bf16[8,64,896]{2,1,0:T(8,128)(2,1)} %broadcast_in_dim.7), calls=%async_computation.3 | async-start | bytes 1835008 | tf_op jit(solution)/shard_map/all_to_all | solution.py:34
  94.4 0.0 collective-permute-done.2
  94.4 10.6 %all-to-all-done.3 = bf16[8,64,896]{2,1,0:T(8,128)(2,1)S(1)} async-done(((bf16[8,64,896]{2,1,0:T(8,128)(2,1)}), bf16[8,64,896]{2,1,0:T(8,128)(2,1)S(1)}, u32[]{:S(2)}, u32[]{:S(2)}) %all-to-all-start.3) | async-done | bytes 917536 | tf_op jit(solution)/shard_map/all_to_all | solution.py:34
  105.0 2.4 %fusion.12 = bf16[512,1024]{1,0:T(8,128)(2,1)S(1)} fusion(bf16[512,896]{1,0:T(8,128)(2,1)S(1)} %bitcast.21, bf16[448,1024]{1,0:T(8,128)(2,1)} %collective-permute-done.2, bf16[448,1024]{1,0:T(8,128)(2,1)S(1)} %copy-done.2), kind=kOutput, calls=%fused_computation.14 | convolution fusion | flops 943718400 | bytes 3801088 | tf_op jit(solution)/shard_map/dot_general | solution.py:13
  107.4 0.1 copy.8
  107.5 36.7 %all_to_all.30 = bf16[8,64,1024]{2,1,0:T(8,128)(2,1)S(1)} all-to-all(bf16[8,64,1024]{2,1,0:T(8,128)(2,1)S(1)} %bitcast.16), channel_id=1, replica_groups=mesh['zh'=4,'zl'=4,'xh'=2,'core'=2,'xl'=2,'y'=4] {'zl','xh'}, dimensions={0} | all-to-all | bytes 2097152 | tf_op jit(solution)/shard_map/all_to_all | solution.py:40
  144.2 0.2 reduce_sum.34
  144.4 27.0 %all_to_all.31 = bf16[4,16,1024]{2,1,0:T(8,128)(2,1)S(1)} all-to-all(bf16[4,16,1024]{2,1,0:T(8,128)(2,1)S(1)} %bitcast.22), channel_id=1, replica_groups=mesh['zh'=4,'zl'=4,'xh'=2,'core'=2,'xl'=2,'y'=4] {'zh'}, dimensions={0} | all-to-all | bytes 262144 | tf_op jit(solution)/shard_map/all_to_all | solution.py:42
  171.4 0.6 reduce_sum.35
Async XLA Ops:
  1.6 44.3 %all-to-all-start = ((bf16[16,16,1024]{2,1,0:T(8,128)(2,1)}), bf16[16,16,1024]{2,1,0:T(8,128)(2,1)S(1)}, u32[]{:S(2)}, u32[]{:S(2)}) async-start(bf16[16,16,1024]{2,1,0:T(8,128)(2,1)} %stack.2), calls=%async_computation | async-start | bytes 1048576 | tf_op jit(solution)/shard_map/all_to_all | solution.py:20
  16.8 33.8 %collective-permute-start = (bf16[1024,448]{0,1:T(8,128)(2,1)}, bf16[1024,448]{0,1:T(8,128)(2,1)}, u32[]{:S(2)}, u32[]{:S(2)}) collective-permute-start(bf16[1024,448]{0,1:T(8,128)(2,1)} %param.5), channel_id=1, source_target_pairs={{0,8},{8,0},{1,9},{9,1},{2,10},{10,2},{3,11},{11,3},{4,12},{12,4},... | collective-permute-start | bytes 2752520 | tf_op jit(solution)/shard_map/ppermute | solution.py:17
  18.7 45.1 %collective-permute-start.1 = (bf16[1024,448]{0,1:T(8,128)(2,1)}, bf16[1024,448]{0,1:T(8,128)(2,1)S(1)}, u32[]{:S(2)}, u32[]{:S(2)}) collective-permute-start(bf16[1024,448]{0,1:T(8,128)(2,1)} %param.6), channel_id=1, source_target_pairs={{0,8},{8,0},{1,9},{9,1},{2,10},{10,2},{3,11},{11,3},{4,12},{12,4},... | collective-permute-start | bytes 2752520 | tf_op jit(solution)/shard_map/ppermute | solution.py:18
  45.9 15.6 %copy-start = (bf16[1024,448]{0,1:T(8,128)(2,1)S(1)}, bf16[1024,448]{0,1:T(8,128)(2,1)}, u32[]{:S(2)}) copy-start(bf16[1024,448]{0,1:T(8,128)(2,1)} %param.5) | copy-start | bytes 2752516
  47.0 14.5 %all-to-all-start.1 = ((bf16[2,256,1024]{2,1,0:T(8,128)(2,1)}), bf16[2,256,1024]{2,1,0:T(8,128)(2,1)S(1)}, u32[]{:S(2)}, u32[]{:S(2)}) async-start(bf16[2,256,1024]{2,1,0:T(8,128)(2,1)} %broadcast_in_dim.6), calls=%async_computation.1 | async-start | bytes 2097152 | tf_op jit(solution)/shard_map/all_to_all | solution.py:21
  61.5 2.4 %copy-start.1 = (bf16[1024,448]{0,1:T(8,128)(2,1)S(1)}, bf16[1024,448]{0,1:T(8,128)(2,1)}, u32[]{:S(2)}) copy-start(bf16[1024,448]{0,1:T(8,128)(2,1)} %param.6) | copy-start | bytes 2752516
  67.7 6.1 %copy-start.2 = (bf16[448,1024]{1,0:T(8,128)(2,1)S(1)}, bf16[448,1024]{1,0:T(8,128)(2,1)}, u32[]{:S(2)}) copy-start(bf16[448,1024]{1,0:T(8,128)(2,1)} %param.7) | copy-start | bytes 2752516
  67.7 21.0 %all-to-all-start.2 = ((bf16[8,64,1792]{2,1,0:T(8,128)(2,1)}), bf16[8,64,1792]{2,1,0:T(8,128)(2,1)S(1)}, u32[]{:S(2)}, u32[]{:S(2)}) async-start(bf16[8,64,1792]{2,1,0:T(8,128)(2,1)} %bitcast.4), calls=%async_computation.2 | async-start | bytes 3670016 | tf_op jit(solution)/shard_map/all_to_all | solution.py:31
  73.7 20.7 %collective-permute-start.2 = (bf16[448,1024]{1,0:T(8,128)(2,1)S(1)}, bf16[448,1024]{1,0:T(8,128)(2,1)}, u32[]{:S(2)}, u32[]{:S(2)}) collective-permute-start(bf16[448,1024]{1,0:T(8,128)(2,1)S(1)} %copy-done.2), channel_id=1, source_target_pairs={{0,8},{8,0},{1,9},{9,1},{2,10},{10,2},{3,11},{11,3},{4,12},{12,4},... | collective-permute-start | bytes 2752520 | tf_op jit(solution)/shard_map/ppermute | solution.py:19
  90.1 14.9 %all-to-all-start.3 = ((bf16[8,64,896]{2,1,0:T(8,128)(2,1)}), bf16[8,64,896]{2,1,0:T(8,128)(2,1)S(1)}, u32[]{:S(2)}, u32[]{:S(2)}) async-start(bf16[8,64,896]{2,1,0:T(8,128)(2,1)} %broadcast_in_dim.7), calls=%async_computation.3 | async-start | bytes 1835008 | tf_op jit(solution)/shard_map/all_to_all | solution.py:34
